TPU v7x, 32 devices: a whole 2x2x4 slice. The times are simulated.
32 devices in a mesh: groups: 2 (over x), dp: 16 (over z, y, core).
Axes of the slice: x: 2, y: 2, z: 4, core: 2. Of those that a mesh axis runs over, the one named last changes fastest.
Arguments:
- inputs: bfloat16 [64, 128, 4096], P(('groups', 'dp')), parts along dimension 0, may hold values from -6 to 6
- outputs: bfloat16 [64, 128, 4096], P(('groups', 'dp')), parts along dimension 0, may hold values from -6 to 6
- lengths: int32 [64], P(('groups', 'dp')), parts along dimension 0, may hold values from 64 to 128
- labels: int32 [64], P(('groups', 'dp')), parts along dimension 0, may hold values from 0 to 13
- norm_gain: float32 [4096], replicated, may hold values from 0.1 to 1.9
- classifier: bfloat16 [4096, 14], replicated, may hold values from -0.09375 to 0.09375
- proj_in: bfloat16 [4096, 64], replicated, may hold values from -0.09375 to 0.09375
- proj_out: bfloat16 [4096, 128], replicated, may hold values from -0.09375 to 0.09375
- query_index: int32 [256], P('groups'), parts along dimension 0, may hold values from 0 to 31, as said below
- prior_fisher: float32 [16384, 8192], P('groups', 'dp'), parts along dimension 0, may hold values from -4 to 18, as said below
Outputs:
- influence: float32 [8192, 256], P('dp', 'groups'), parts along dimension 1
- scores: float32 [64, 128], P(('groups', 'dp')), parts along dimension 0
There are 2 independent parts, one for each index of `groups`. A program takes and returns all parts, laid end to end along the dimension named above; an argument that names none is the same for every part. Nothing has to cross between parts.
Inputs may be any that keep to these rules, and one draw needn't show every extreme that they name: `query_index`: indices may repeat. `prior_fisher`: symmetric and positive definite.
All inputs are finite; a program needn't handle non-finite values.
Results may differ from a plain program's by a relative error of at most 0.0044.
Values may be sent and summed in bfloat16 or wider, within the bound.
A program may use at most 128 MiB of HBM per device.

v0:
```python
import jax
import jax.numpy as jnp
from jax import lax
from jax.sharding import PartitionSpec as P

D = 4096
CLASSES = 14
ITERS = 4


norm_eps = 1e-05
damp_share = 0.5
highest = lax.Precision.HIGHEST


def project_rows(inputs, outputs, lengths, labels, norm_gain, classifier, proj_in, proj_out):
    ex_count = inputs.shape[0]
    tok_count = inputs.shape[1]
    hidden = outputs.astype(jnp.float32)
    root_mean = jnp.sqrt(jnp.mean(hidden * hidden, axis=-1, keepdims=True) + norm_eps)
    positions = jnp.arange(tok_count, dtype=jnp.int32)
    live_mask = (positions[None, :] < lengths[:, None]).astype(jnp.float32)[:, :, None]
    length_float = lengths.astype(jnp.float32)[:, None, None]
    normed = norm_gain * hidden / root_mean
    pooled = jnp.sum(live_mask * normed, axis=1) / length_float[:, 0]
    class_weight = classifier.astype(jnp.float32)
    logits = jnp.dot(pooled, class_weight, precision=highest)
    exponent = jnp.exp(logits)
    probs = exponent / jnp.sum(exponent, axis=-1, keepdims=True)
    target = (jnp.arange(CLASSES, dtype=jnp.int32)[None, :] == labels[:, None]).astype(jnp.float32)
    pooled_grad = lax.dot_general(
        probs - target, class_weight, (((1,), (1,)), ((), ())), precision=highest
    )
    scaled = norm_gain * (live_mask / length_float) * pooled_grad[:, None, :]
    out_grad = scaled / root_mean - hidden * jnp.sum(hidden * scaled, axis=-1, keepdims=True) / (
        D * root_mean**3
    )
    grad_low = out_grad.astype(jnp.bfloat16)
    input_proj = jnp.dot(
        inputs.reshape(ex_count * tok_count, D).astype(jnp.float32),
        proj_in.astype(jnp.float32),
        precision=highest,
    )
    grad_proj = jnp.dot(
        grad_low.reshape(ex_count * tok_count, D).astype(jnp.float32),
        proj_out.astype(jnp.float32),
        precision=highest,
    )
    input_proj = input_proj.reshape(ex_count, tok_count, -1)
    grad_proj = grad_proj.reshape(ex_count, tok_count, -1)
    outer = jnp.einsum("eta,etb->eab", input_proj, grad_proj, precision=highest)
    return outer.reshape(ex_count, -1).astype(jnp.bfloat16)


def conjugate(queries, apply_fisher, reduce_inner):
    solved = jnp.zeros_like(queries)
    residual = queries
    direction = queries
    norm_now = reduce_inner(residual, residual)
    for step_index in range(ITERS):
        image = apply_fisher(direction)
        alpha = norm_now / reduce_inner(direction, image)
        solved = solved + alpha * direction
        residual = residual - alpha * image
        norm_next = reduce_inner(residual, residual)
        direction = residual + norm_next / norm_now * direction
        norm_now = norm_next
    return solved


def pieces_inner(first_vec, second_vec):
    return lax.psum(jnp.sum(first_vec * second_vec, axis=0), "dp")


def contract_rows(left_rows, right_rows):
    return jnp.dot(
        left_rows.astype(jnp.float32).T, right_rows.astype(jnp.float32), precision=highest
    )


def body(
    inputs,
    outputs,
    lengths,
    labels,
    norm_gain,
    classifier,
    proj_in,
    proj_out,
    query_index,
    prior_fisher,
):
    own_rows = project_rows(
        inputs, outputs, lengths, labels, norm_gain, classifier, proj_in, proj_out
    )
    devices = lax.axis_size("dp")
    device_index = lax.axis_index("dp")
    own_count = own_rows.shape[0]
    total_rows = own_count * devices
    width = own_rows.shape[1]
    piece = width // devices
    own_float = own_rows.astype(jnp.float32)
    square_sum = lax.psum(jnp.sum(own_float * own_float), "dp")
    damping = damp_share * square_sum / (total_rows * total_rows)
    every = lax.all_gather(own_rows, "dp", axis=0, tiled=True)
    mine = lax.dynamic_slice_in_dim(every, device_index * piece, piece, 1)
    strip = contract_rows(every, mine) / total_rows + damping * prior_fisher

    def apply_piece(vectors):
        return lax.psum_scatter(
            jnp.dot(strip, vectors, precision=highest), "dp", scatter_dimension=0, tiled=True
        )

    queries = jnp.take(mine, query_index, axis=0).astype(jnp.float32).T
    solved = conjugate(queries, apply_piece, pieces_inner)
    block = mine.astype(jnp.float32)
    scores = lax.psum_scatter(
        jnp.dot(block, solved, precision=highest) / total_rows,
        "dp",
        scatter_dimension=0,
        tiled=True,
    )
    return (solved, scores)


def solution(mesh):
    return jax.shard_map(
        body,
        mesh=mesh,
        in_specs=(
            P(("groups", "dp"), None, None),
            P(("groups", "dp"), None, None),
            P(("groups", "dp")),
            P(("groups", "dp")),
            P(),
            P(),
            P(),
            P(),
            P("groups"),
            P("groups", "dp"),
        ),
        out_specs=(P("dp", "groups"), P(("groups", "dp"), None)),
        check_vma=False,
    )
```

profile of v0, /device:TPU:0, one launch (start us, length us, event | category | flops | bytes accessed | tf_op | source)
XLA Modules:
  0.0 715.0 jit_solution(6194514816210829395)
XLA Ops:
  7.3 0.8 convert_element_type.49
  8.1 0.8 compare_convert_fusion.1
  8.9 0.7 compare_select_fusion
  9.6 0.7 compare_and_fusion
  10.2 2.1 fusion.6
  12.3 0.7 add_sqrt_fusion
  13.1 2.5 fusion.8
  15.6 0.4 fusion.33
  16.0 0.3 fusion.25
  16.3 2.1 fusion.3
  18.4 0.7 fusion.12
  19.2 0.8 fusion.14
  19.9 0.8 multiply_reduce_fusion.6
  20.8 24.6 %all-gather = bf16[16,2,8192]{2,1,0:T(2,128)(2,1)S(1)} all-gather(bf16[1,2,8192]{2,1,0:T(2,128)(2,1)S(1)} %reshape.115), channel_id=1, replica_groups=mesh['groups'=2,'dp'=16] {'dp'}, dimensions={0}, use_global_device_ids=true | all-gather | bytes 557056 | tf_op jit(solution)/shard_map/all_gather | solution.py:105
  45.4 0.2 reshape.116
  45.6 30.5 %psum.64 = f32[]{:T(128)} all-reduce(f32[]{:T(128)} %get-tuple-element.12), channel_id=1, replica_groups=mesh['groups'=2,'dp'=16] {'dp'}, use_global_device_ids=true, to_apply=%region_7.8 | all-reduce | flops 1 | bytes 8 | tf_op jit(solution)/shard_map/psum | solution.py:103
  76.1 0.8 gather_fusion
  77.7 8.1 %multiply_add_fusion = f32[8192,512]{1,0:T(8,128)S(1)} fusion(f32[8192,512]{1,0:T(8,128)} %param.19, bf16[32,8192]{1,0:T(8,128)(2,1)S(1)} %reshape.116, bf16[32,512]{1,0:T(8,128)(2,1)S(1)} %constant_dynamic-slice_fusion.1, f32[]{:T(128)S(6)} %div.104), kind=kOutput, calls=%fused_computation.2 | convolution fusion | flops 281018368 | bytes 34111492 | tf_op jit(solution)/shard_map/dot_general | solution.py:76
  85.9 5.7 copy-done.1
  91.6 9.1 %fusion.22 = f32[8192,128]{1,0:T(8,128)} fusion(f32[8192,512]{1,0:T(8,128)S(1)} %multiply_add_fusion, bf16[128,512]{0,1:T(8,128)(2,1)S(1)} %copy.13, pred[128]{0:T(512)(128)(4,1)S(1)} %compare_and_fusion), kind=kOutput, calls=%fused_computation.49 | convolution fusion | flops 6442516480 | bytes 21102720 | tf_op jit(solution)/shard_map/dot_general | solution.py:111
  100.7 69.7 %reduce-scatter.5.cloned.1.call-done = f32[512,128]{1,0:T(8,128)} async-done(((f32[8192,128]{1,0:T(8,128)}), f32[512,128]{1,0:T(8,128)}) %reduce-scatter.5.cloned.1.call-update) | async-done | bytes 262160 | tf_op jit(solution)/shard_map/reduce_scatter | solution.py:110
  170.5 1.0 fusion.17
  171.5 30.4 %all-reduce.1 = (f32[128]{0:T(128)S(1)}, f32[128]{0:T(128)S(1)}) all-reduce(f32[128]{0:T(128)S(1)} %get-tuple-element.3, f32[128]{0:T(128)S(1)} %get-tuple-element.2), channel_id=1, replica_groups=mesh['groups'=2,'dp'=16] {'dp'}, use_global_device_ids=true, to_apply=%region_5.0 | all-reduce | flops 256 | bytes 2048 | tf_op jit(solution)/shard_map/psum | solution.py:72
  201.9 1.0 multiply_reduce_fusion.5
  202.9 29.5 %psum.66 = f32[128]{0:T(128)S(1)} all-reduce(f32[128]{0:T(128)S(1)} %multiply_reduce_fusion.5), channel_id=1, replica_groups=mesh['groups'=2,'dp'=16] {'dp'}, use_global_device_ids=true, to_apply=%region_12.13 | all-reduce | flops 128 | bytes 1024 | tf_op jit(solution)/shard_map/psum | solution.py:72
  232.4 17.4 %fusion.31 = f32[8192,128]{1,0:T(8,128)} fusion(f32[8192,512]{1,0:T(8,128)} %copy-done.1, f32[512,128]{1,0:T(8,128)} %reduce-scatter.5.cloned.1.call-done, f32[128]{0:T(128)S(1)} %div.106, f32[128]{0:T(128)S(1)} %div.105, bf16[128,512]{0,1:T(8,128)(2,1)S(1)} %copy.13, pred[128]{0:T(512)(128)(4,1)S(1)} %compare_and_fusion), kind=kOutput, calls=%fused_computation.69 | convolution fusion | flops 6442844160 | bytes 21365888 | tf_op jit(solution)/shard_map/dot_general | solution.py:111
  249.9 69.6 %reduce-scatter.7.cloned.1.call-done = f32[512,128]{1,0:T(8,128)} async-done(((f32[8192,128]{1,0:T(8,128)}), f32[512,128]{1,0:T(8,128)}) %reduce-scatter.7.cloned.1.call-update) | async-done | bytes 262160 | tf_op jit(solution)/shard_map/reduce_scatter | solution.py:110
  319.5 1.0 multiply_reduce_fusion.4
  320.6 30.1 %psum.67 = f32[128]{0:T(128)S(1)} all-reduce(f32[128]{0:T(128)S(1)} %multiply_reduce_fusion.4), channel_id=1, replica_groups=mesh['groups'=2,'dp'=16] {'dp'}, use_global_device_ids=true, to_apply=%region_15.16 | all-reduce | flops 128 | bytes 1024 | tf_op jit(solution)/shard_map/psum | solution.py:72
  350.7 1.0 multiply_reduce_fusion.3
  351.8 29.5 %psum.68 = f32[128]{0:T(128)S(1)} all-reduce(f32[128]{0:T(128)S(1)} %get-tuple-element.6), channel_id=1, replica_groups=mesh['groups'=2,'dp'=16] {'dp'}, use_global_device_ids=true, to_apply=%region_17.18 | all-reduce | flops 128 | bytes 1024 | tf_op jit(solution)/shard_map/psum | solution.py:72
  381.4 17.4 %fusion.34 = f32[8192,128]{1,0:T(8,128)} fusion(f32[8192,512]{1,0:T(8,128)} %copy-done.1, f32[512,128]{1,0:T(8,128)S(1)} %multiply_add_fusion.2), kind=kOutput, calls=%fused_computation.71 | convolution fusion | flops 6442450944 | bytes 21233664 | tf_op jit(solution)/shard_map/dot_general | solution.py:111
  398.8 69.7 %reduce-scatter.9.cloned.1.call-done = f32[512,128]{1,0:T(8,128)} async-done(((f32[8192,128]{1,0:T(8,128)}), f32[512,128]{1,0:T(8,128)}) %reduce-scatter.9.cloned.1.call-update) | async-done | bytes 262160 | tf_op jit(solution)/shard_map/reduce_scatter | solution.py:110
  468.6 1.0 multiply_reduce_fusion.2
  469.6 30.1 %psum.69 = f32[128]{0:T(128)S(1)} all-reduce(f32[128]{0:T(128)S(1)} %multiply_reduce_fusion.2), channel_id=1, replica_groups=mesh['groups'=2,'dp'=16] {'dp'}, use_global_device_ids=true, to_apply=%region_20.21 | all-reduce | flops 128 | bytes 1024 | tf_op jit(solution)/shard_map/psum | solution.py:72
  499.7 1.0 multiply_reduce_fusion.1
  500.8 29.7 %psum.70 = f32[128]{0:T(128)S(1)} all-reduce(f32[128]{0:T(128)S(1)} %multiply_reduce_fusion.1), channel_id=1, replica_groups=mesh['groups'=2,'dp'=16] {'dp'}, use_global_device_ids=true, to_apply=%region_22.23 | all-reduce | flops 128 | bytes 1024 | tf_op jit(solution)/shard_map/psum | solution.py:72
  530.5 1.0 multiply_add_fusion.1
  531.5 17.4 %fusion.35 = f32[8192,128]{1,0:T(8,128)} fusion(f32[8192,512]{1,0:T(8,128)} %copy-done.1, f32[512,128]{1,0:T(8,128)S(1)} %multiply_add_fusion.1), kind=kOutput, calls=%fused_computation.72 | convolution fusion | flops 6442450944 | bytes 21233664 | tf_op jit(solution)/shard_map/dot_general | solution.py:111
  548.9 0.6 copy-done.10
  549.6 0.6 dynamic-slice
  550.8 68.0 %reduce-scatter.11.cloned.1.call-done = f32[512,128]{1,0:T(8,128)} async-done(((f32[8192,128]{1,0:T(8,128)}), f32[512,128]{1,0:T(8,128)}) %reduce-scatter.11.cloned.1.call-update) | async-done | bytes 262160 | tf_op jit(solution)/shard_map/reduce_scatter | solution.py:110
  618.8 1.0 multiply_reduce_fusion
  619.9 30.1 %psum.71 = f32[128]{0:T(128)S(1)} all-reduce(f32[128]{0:T(128)S(1)} %multiply_reduce_fusion), channel_id=1, replica_groups=mesh['groups'=2,'dp'=16] {'dp'}, use_global_device_ids=true, to_apply=%region_25.26 | all-reduce | flops 128 | bytes 1024 | tf_op jit(solution)/shard_map/psum | solution.py:72
  649.9 0.1 fusion.20
  650.1 0.2 convolution_multiply_fusion
  650.3 57.6 %all-reduce = f32[32,128]{1,0:T(8,128)S(1)} all-reduce(f32[32,128]{1,0:T(8,128)S(1)} %convolution_multiply_fusion), channel_id=6, replica_groups=mesh['groups'=2,'dp'=16] {'dp'}, use_global_device_ids=true, to_apply=%region_26.27.clone | all-reduce | flops 4096 | bytes 32768
  707.9 0.6 constant_dynamic-slice_fusion
  (40 shorter events, 0.6 us)
Async XLA Ops:
  7.2 12.0 %copy-start = (bf16[2,128,4096]{2,1,0:T(8,128)(2,1)S(1)}, bf16[2,128,4096]{2,1,0:T(8,128)(2,1)}, u32[]{:S(2)}) copy-start(bf16[2,128,4096]{2,1,0:T(8,128)(2,1)} %param.10) | copy-start | bytes 6291460
  7.2 9.1 %copy-start.7 = (f32[4096]{0:T(1024)S(1)}, f32[4096]{0:T(1024)}, u32[]{:S(2)}) copy-start(f32[4096]{0:T(1024)} %param.14) | copy-start | bytes 49156
  7.2 8.4 %copy-start.8 = (bf16[4096,14]{0,1:T(8,128)(2,1)S(1)}, bf16[4096,14]{0,1:T(8,128)(2,1)}, u32[]{:S(2)}) copy-start(bf16[4096,14]{0,1:T(8,128)(2,1)} %param.15) | copy-start | bytes 344068
  7.2 8.8 %copy-start.9 = (s32[2]{0:T(128)S(1)}, s32[2]{0:T(128)}, u32[]{:S(2)}) copy-start(s32[2]{0:T(128)} %param.13) | copy-start | bytes 28
  7.2 163.2 %reduce-scatter.5.cloned.1.call-start = ((), (), s32[]{:S(2)}) async-start(), calls=%async_computation.4 | async-start | bytes 4456448 | tf_op jit(solution)/shard_map/reduce_scatter | solution.py:110
  7.3 9.1 %copy-start.3 = (bf16[2,128,4096]{2,1,0:T(8,128)(2,1)S(1)}, bf16[2,128,4096]{2,1,0:T(8,128)(2,1)}, u32[]{:S(2)}) copy-start(bf16[2,128,4096]{2,1,0:T(8,128)(2,1)} %param.11) | copy-start | bytes 6291460
  16.3 2.1 copy-start.4
  16.3 2.8 copy-start.6
  85.8 5.7 copy-start.1
  100.7 218.9 %reduce-scatter.7.cloned.1.call-start = ((), (), s32[]{:S(2)}) async-start(), calls=%async_computation.5 | async-start | bytes 4456448 | tf_op jit(solution)/shard_map/reduce_scatter | solution.py:110
  249.8 69.7 %copy-start.2 = (f32[512,128]{1,0:T(8,128)S(1)}, f32[512,128]{1,0:T(8,128)}, u32[]{:S(2)}) copy-start(f32[512,128]{1,0:T(8,128)} %reduce-scatter.5.cloned.1.call-done) | copy-start | bytes 786436
  249.8 218.7 %reduce-scatter.9.cloned.1.call-start = ((), (), s32[]{:S(2)}) async-start(), calls=%async_computation.6 | async-start | bytes 4456448 | tf_op jit(solution)/shard_map/reduce_scatter | solution.py:110
  398.8 220.0 %reduce-scatter.11.cloned.1.call-start = ((), (), s32[]{:S(2)}) async-start(), calls=%async_computation.7 | async-start | bytes 4456448 | tf_op jit(solution)/shard_map/reduce_scatter | solution.py:110
  548.9 0.7 copy-start.10
  650.0 58.4 %copy-start.5 = (f32[512,128]{1,0:T(8,128)}, f32[512,128]{1,0:T(8,128)S(1)}, u32[]{:S(2)}) copy-start(f32[512,128]{1,0:T(8,128)S(1)} %fusion.20) | copy-start | bytes 786436
Sparse Core Ops, SparseCore 0:
  100.8 69.6 reduce-scatter.4
  250.0 69.5 reduce-scatter.6
  398.9 69.6 reduce-scatter.8
  549.1 69.7 reduce-scatter.10
where the time goes:
time: 716 us; the launch traced here: 715 us
  blocking collectives  322 us (45%)
  waiting for transfers between devices  277 us (39%)
  matrix products  72.7 us (10%)
  other arithmetic  18.8 us (3%)
  between operations  15.3 us (2%)
  local copies, waits for them, and re-layouts  8.71 us (1%)
    reduce_scatter x4, waiting for transfers between devices, apply_piece(): lax.psum_scatter(jnp.dot(strip, vectors, precision=highest), 'dp', scatte...  277 us
    psum x7, blocking collectives, pieces_inner(): return lax.psum(jnp.sum(first_vec * second_vec, axis=0), 'dp')  209 us
    dot_general x4, matrix products, apply_piece(): jnp.dot(strip, vectors, precision=highest)  61.4 us
    unnamed x1, blocking collectives  57.6 us
    psum x1, blocking collectives, body(): square_sum = lax.psum(jnp.sum(own_float * own_float), 'dp')  30.5 us
    all_gather x1, blocking collectives, body(): every = lax.all_gather(own_rows, 'dp', axis=0, tiled=True)  24.6 us
  transfers between devices with their start and end apart: 4, of which 4 were waited for; matrix products, arithmetic and copies ran while one was open for 0% of the time, Pallas kernels for 0%

commit v1 on v0

v1 whole, which is shorter than its diff:
```python
import functools

import jax
import jax.numpy as jnp
from jax import lax
from jax.experimental import pallas as pl
from jax.experimental.pallas import tpu as pltpu
from jax.sharding import PartitionSpec as P

D = 4096
CLASSES = 14
ITERS = 4


norm_eps = 1e-05
damp_share = 0.5
highest = lax.Precision.HIGHEST


def project_rows(inputs, outputs, lengths, labels, norm_gain, classifier, proj_in, proj_out):
    ex_count = inputs.shape[0]
    tok_count = inputs.shape[1]
    hidden = outputs.astype(jnp.float32)
    root_mean = jnp.sqrt(jnp.mean(hidden * hidden, axis=-1, keepdims=True) + norm_eps)
    positions = jnp.arange(tok_count, dtype=jnp.int32)
    live_mask = (positions[None, :] < lengths[:, None]).astype(jnp.float32)[:, :, None]
    length_float = lengths.astype(jnp.float32)[:, None, None]
    normed = norm_gain * hidden / root_mean
    pooled = jnp.sum(live_mask * normed, axis=1) / length_float[:, 0]
    class_weight = classifier.astype(jnp.float32)
    logits = jnp.dot(pooled, class_weight, precision=highest)
    exponent = jnp.exp(logits)
    probs = exponent / jnp.sum(exponent, axis=-1, keepdims=True)
    target = (jnp.arange(CLASSES, dtype=jnp.int32)[None, :] == labels[:, None]).astype(jnp.float32)
    pooled_grad = lax.dot_general(
        probs - target, class_weight, (((1,), (1,)), ((), ())), precision=highest
    )
    scaled = norm_gain * (live_mask / length_float) * pooled_grad[:, None, :]
    out_grad = scaled / root_mean - hidden * jnp.sum(hidden * scaled, axis=-1, keepdims=True) / (
        D * root_mean**3
    )
    grad_low = out_grad.astype(jnp.bfloat16)
    input_proj = jnp.dot(
        inputs.reshape(ex_count * tok_count, D),
        proj_in,
        preferred_element_type=jnp.float32,
    )
    grad_proj = jnp.dot(
        grad_low.reshape(ex_count * tok_count, D),
        proj_out,
        preferred_element_type=jnp.float32,
    )
    input_proj = input_proj.reshape(ex_count, tok_count, -1)
    grad_proj = grad_proj.reshape(ex_count, tok_count, -1)
    outer = jnp.einsum("eta,etb->eab", input_proj, grad_proj, precision=highest)
    return outer.astype(jnp.bfloat16)


BASIS_SCALE = 0.125
STAGES = 4
BUFFERS = 4


def solve_kernel(
    devices,
    rows_ref,
    query_ref,
    prior_ref,
    influence_ref,
    scores_ref,
    rows_all,
    rows_wide,
    vectors,
    own_vectors,
    prior_low,
    staging,
    small,
    row_send,
    row_pass,
    row_recv,
    vec_send,
    vec_pass,
    vec_recv,
    small_send,
    small_recv,
    stage_sem,
):
    me = lax.axis_index("dp")
    chips = devices // 2
    chip = me // 2
    core = lax.rem(me, 2)
    sibling = chip * 2 + 1 - core
    own_count, feat_in, feat_out = rows_ref.shape
    total = own_count * devices
    width, piece = prior_ref.shape
    span = 4 * total
    groups_in = feat_in // devices

    def load(step):
        block = lax.rem(me + step, devices)
        return pltpu.make_async_copy(
            prior_ref.at[pl.ds(pl.multiple_of(block * piece, piece), piece)],
            staging.at[lax.rem(step, BUFFERS)],
            stage_sem.at[lax.rem(step, BUFFERS)],
        )

    for step in range(BUFFERS):
        load(step).start()

    barrier = pltpu.get_barrier_semaphore()

    def greet(step, carry):
        pl.semaphore_signal(
            barrier, inc=1, device_id={"dp": lax.rem(me + step, devices)}
        )
        return carry

    lax.fori_loop(1, devices, greet, 0)
    pl.semaphore_wait(barrier, devices - 1)

    def send(view, sem_out, sem_in, target):
        return pltpu.make_async_remote_copy(
            src_ref=view,
            dst_ref=view,
            send_sem=sem_out,
            recv_sem=sem_in,
            device_id={"dp": target},
        )

    def row_view(source):
        return rows_all.at[pl.ds(source * own_count, own_count)]

    def row_copy(source, sem_out, target):
        return send(row_view(source), sem_out, row_recv.at[source], target)

    def vec_copy(stage, source, sem_out, target):
        view = vectors.at[source, pl.ds(stage * total, total)]
        return send(view, sem_out, vec_recv.at[stage, source], target)

    def near(step):
        return lax.rem(chip + chips - step, chips) * 2 + core

    def far(step):
        return lax.rem(chip + chips - step, chips) * 2 + 1 - core

    def ahead(step):
        return lax.rem(chip + step, chips) * 2 + core

    def gather(copy, out_sems, pass_sems, use, state):
        copy(me, out_sems(0), sibling).start()

        def push(step, carry):
            copy(me, out_sems(step), ahead(step)).start()
            return carry

        lax.fori_loop(1, chips, push, 0)
        state = use(me, state)

        def take_near(step, carry):
            source = near(step)
            copy(source, out_sems(step), ahead(step)).wait_recv()
            copy(source, pass_sems(step), sibling).start()
            return use(source, carry)

        state = lax.fori_loop(1, chips, take_near, state)

        def take_far(step, carry):
            source = far(step)
            copy(source, out_sems(0), sibling).wait_recv()
            return use(source, carry)

        return lax.fori_loop(0, chips, take_far, state)

    def drain(copy, out_sems, pass_sems):
        copy(me, out_sems(0), sibling).wait_send()

        def finish(step, carry):
            copy(me, out_sems(step), ahead(step)).wait_send()
            copy(near(step), pass_sems(step), sibling).wait_send()
            return carry

        lax.fori_loop(1, chips, finish, 0)

    def small_copy(turn, step, source, target):
        return send(
            small.at[turn, source], small_send.at[turn, step], small_recv.at[turn, source], target
        )

    def small_push(turn):
        def push(step, carry):
            small_copy(turn, step, me, lax.rem(me + step, devices)).start()
            return carry

        lax.fori_loop(1, devices, push, 0)

    def small_sum(turn):
        def finish(step, carry):
            source = lax.rem(me + devices - step, devices)
            small_copy(turn, step, source, source).wait_recv()
            small_copy(turn, step, me, source).wait_send()
            return carry

        lax.fori_loop(1, devices, finish, 0)
        return jnp.sum(small[turn], axis=0)

    rows_all[pl.ds(me * own_count, own_count)] = rows_ref[...]
    row_sems = (row_copy, lambda step: row_send.at[step], lambda step: row_pass.at[step])

    def cast_first():
        load(0).wait()
        block = staging[0]
        row_ids = lax.broadcasted_iota(jnp.int32, (piece, piece), 0)
        col_ids = lax.broadcasted_iota(jnp.int32, (piece, piece), 1)
        on_diag = row_ids == col_ids
        diag = jnp.sum(jnp.where(on_diag, block, 0.0), axis=0, keepdims=True)
        prior_low[me] = jnp.where(on_diag, 0.0, block).astype(jnp.bfloat16)
        load(BUFFERS).start()
        return diag

    diag = cast_first()
    mean_diag = jnp.sum(diag) / width
    small[0, me] = jnp.full(small.shape[2:], mean_diag, jnp.float32)
    small_push(0)

    def cast(step, carry):
        load(step).wait()
        prior_low[lax.rem(me + step, devices)] = staging[lax.rem(step, BUFFERS)].astype(
            jnp.bfloat16
        )

        @pl.when(step + BUFFERS < devices)
        def _():
            load(step + BUFFERS).start()

        return carry

    def use_rows(source, step):
        @pl.when(step > 0)
        def _():
            cast(step, 0)

        return step + 1

    gather(*row_sems, use_rows, 0)

    def widen(step, carry):
        rows_wide[pl.ds(pl.multiple_of(step * feat_in, feat_in), feat_in)] = rows_all[
            step
        ].astype(jnp.float32)
        return carry

    lax.fori_loop(0, total, widen, 0)
    for index in range(feat_in):
        vectors[
            index // groups_in,
            0:total,
            (index % groups_in) * feat_out : (index % groups_in + 1) * feat_out,
        ] = rows_wide[pl.ds(index, total, stride=feat_in), :].astype(jnp.bfloat16)

    shift = small_sum(0)[0:1, 0:1]
    diag = diag - shift

    def partial(stage):
        def use(source, acc):
            return acc + jnp.dot(
                vectors[source, stage * total : (stage + 1) * total, :],
                prior_low[source],
                preferred_element_type=jnp.float32,
            )

        return use

    def next_vector(stage, acc):
        return BASIS_SCALE * (acc + diag * own_vectors[stage * total : (stage + 1) * total, :])

    zero = jnp.zeros((total, piece), jnp.float32)
    own_vectors[0:total, :] = vectors[me, 0:total, :].astype(jnp.float32)
    acc = lax.fori_loop(0, devices, partial(0), zero)
    for stage in range(1, STAGES):
        fresh = next_vector(stage - 1, acc)
        own_vectors[stage * total : (stage + 1) * total, :] = fresh
        vectors[me, stage * total : (stage + 1) * total, :] = fresh.astype(jnp.bfloat16)
        acc = gather(
            functools.partial(vec_copy, stage),
            lambda step, stage=stage: vec_send.at[stage, step],
            lambda step, stage=stage: vec_pass.at[stage, step],
            partial(stage),
            zero,
        )
    last = next_vector(STAGES - 1, acc)
    product = last * own_vectors[3 * total :, :]
    small[1, me] = lax.dot_general(
        jnp.ones((8, piece), jnp.float32),
        product,
        (((1,), (1,)), ((), ())),
        precision=highest,
        preferred_element_type=jnp.float32,
    )
    small_push(1)

    def add_gram(source, acc):
        block = vectors[source]
        return acc + lax.dot_general(
            block, block, (((1,), (1,)), ((), ())), preferred_element_type=jnp.float32
        )

    gram = lax.fori_loop(0, devices, add_gram, jnp.zeros((span, span), jnp.float32))

    row_ids = lax.broadcasted_iota(jnp.int32, (span, span), 0)
    col_ids = lax.broadcasted_iota(jnp.int32, (span, span), 1)
    trace = jnp.sum(
        jnp.sum(
            jnp.where((row_ids == col_ids) & (row_ids < total), gram, 0.0), axis=0, keepdims=True
        ),
        axis=1,
        keepdims=True,
    )
    damping = damp_share * trace / (total * total)
    lower = damping * shift
    raise_ = damping / BASIS_SCALE
    lanes = lax.broadcasted_iota(jnp.int32, (total, span), 1)
    start = (lanes == lax.broadcasted_iota(jnp.int32, (total, span), 0)).astype(jnp.float32)
    final_lanes = lanes >= 3 * total

    def shift_up(coeffs):
        return jnp.where(lanes >= total, pltpu.roll(coeffs, total, 1), 0.0)

    def dot32(left, right):
        return jnp.dot(left, right, precision=highest, preferred_element_type=jnp.float32)

    def inner(left, right):
        return jnp.sum(left * right, axis=1, keepdims=True)

    solved = jnp.zeros((total, span), jnp.float32)
    residual = start
    direction = start
    projected = dot32(start, gram)
    norm_now = inner(projected, residual)
    for step in range(ITERS):
        moved = shift_up(direction)
        image = (
            jnp.where(lanes < total, projected / total, 0.0) + lower * direction + raise_ * moved
        )
        energy = inner(projected, image)
        if step == ITERS - 1:
            tail = jnp.where(final_lanes, direction, 0.0)
            energy = energy + raise_ * inner(dot32(moved, gram), tail)
            sevenths = small_sum(1)[0:1, :]
            pick = (
                lax.broadcasted_iota(jnp.int32, (total, total), 0)
                == lax.broadcasted_iota(jnp.int32, (total, total), 1)
            )
            seventh = jnp.sum(jnp.where(pick, sevenths, 0.0), axis=1, keepdims=True)
            energy = energy + raise_ * seventh * inner(tail, tail)
        alpha = norm_now / energy
        solved = solved + alpha * direction
        if step < ITERS - 1:
            residual = residual - alpha * image
            pulled = dot32(residual, gram)
            norm_next = inner(pulled, residual)
            ratio = norm_next / norm_now
            direction = residual + ratio * direction
            projected = pulled + ratio * projected
            norm_now = norm_next

    queries = query_ref.shape[0]
    chosen = (
        query_ref[...] == lax.broadcasted_iota(jnp.int32, (queries, total), 1)
    ).astype(jnp.float32)
    picked = dot32(chosen, solved)
    influence_ref[...] = dot32(picked, own_vectors[...]).T
    own_ids = lax.broadcasted_iota(jnp.int32, (8, span), 0) + me * own_count
    own_rows = (
        (own_ids == lax.broadcasted_iota(jnp.int32, (8, span), 1))
        & (lax.broadcasted_iota(jnp.int32, (8, span), 0) < own_count)
    ).astype(jnp.float32)
    shares = dot32(own_rows, gram)
    scored = lax.dot_general(
        shares,
        picked,
        (((1,), (1,)), ((), ())),
        precision=highest,
        preferred_element_type=jnp.float32,
    )
    scores_ref[...] = scored[0:own_count, :] / total

    drain(*row_sems)
    for stage in range(1, STAGES):
        drain(
            functools.partial(vec_copy, stage),
            lambda step, stage=stage: vec_send.at[stage, step],
            lambda step, stage=stage: vec_pass.at[stage, step],
        )


def solve(own_rows, query_index, prior_fisher):
    devices = lax.axis_size("dp")
    own_count, feat_in, feat_out = own_rows.shape
    width, piece = prior_fisher.shape
    total = own_count * devices
    queries = query_index.shape[0]
    vmem = pl.BlockSpec(memory_space=pltpu.VMEM)
    dma = pltpu.SemaphoreType.DMA
    chips = devices // 2
    return pl.pallas_call(
        functools.partial(solve_kernel, devices),
        out_shape=(
            jax.ShapeDtypeStruct((piece, queries), jnp.float32),
            jax.ShapeDtypeStruct((own_count, queries), jnp.float32),
        ),
        in_specs=[vmem, vmem, pl.BlockSpec(memory_space=pl.ANY)],
        out_specs=(vmem, vmem),
        scratch_shapes=[
            pltpu.VMEM((total, feat_in, feat_out), jnp.bfloat16),
            pltpu.VMEM((total * feat_in, feat_out), jnp.float32),
            pltpu.VMEM((devices, 4 * total, piece), jnp.bfloat16),
            pltpu.VMEM((4 * total, piece), jnp.float32),
            pltpu.VMEM((devices, piece, piece), jnp.bfloat16),
            pltpu.VMEM((BUFFERS, piece, piece), jnp.float32),
            pltpu.VMEM((2, devices, 8, total), jnp.float32),
            dma((chips,)),
            dma((chips,)),
            dma((devices,)),
            dma((STAGES, chips)),
            dma((STAGES, chips)),
            dma((STAGES, devices)),
            dma((2, devices)),
            dma((2, devices)),
            dma((BUFFERS,)),
        ],
        compiler_params=pltpu.CompilerParams(
            collective_id=0, has_side_effects=True, vmem_limit_bytes=50 * 1024 * 1024
        ),
        name="solve",
    )(own_rows, query_index[:, None], prior_fisher)


def body(
    inputs,
    outputs,
    lengths,
    labels,
    norm_gain,
    classifier,
    proj_in,
    proj_out,
    query_index,
    prior_fisher,
):
    own_rows = project_rows(
        inputs, outputs, lengths, labels, norm_gain, classifier, proj_in, proj_out
    )
    return solve(own_rows, query_index, prior_fisher)


def solution(mesh):
    return jax.shard_map(
        body,
        mesh=mesh,
        in_specs=(
            P(("groups", "dp"), None, None),
            P(("groups", "dp"), None, None),
            P(("groups", "dp")),
            P(("groups", "dp")),
            P(),
            P(),
            P(),
            P(),
            P("groups"),
            P("groups", "dp"),
        ),
        out_specs=(P("dp", "groups"), P(("groups", "dp"), None)),
        check_vma=False,
    )
```

time: 716 us -> 74.6 us (0.10)
  blocking collectives: 322 us -> 0 us
  waiting for transfers between devices: 277 us -> 0 us
  matrix products: 72.7 us -> 6.02 us
  Pallas kernels: 0 us -> 59 us
  between operations: 15.3 us -> 0.78 us
  other arithmetic: 18.8 us -> 7.2 us
  local copies, waits for them, and re-layouts: 8.71 us -> 1.42 us
    reduce_scatter x4 -> x0, waiting for transfers between devices: 277 us -> none  [apply_piece(): lax.psum_scatter(jnp.dot(strip, vectors, precision=highest), 'dp', scatte...]
    psum x8 -> x0, blocking collectives: 240 us -> none  [the longest x7 209 us: pieces_inner(): return lax.psum(jnp.sum(first_vec * second_vec, axis=0), 'dp')]
    dot_general x8 -> x2, matrix products: 71.2 us -> 5.09 us  [the longest x1 4.33 us: project_rows(): jnp.dot(grad_low.reshape(ex_count * tok_count, D), proj_out, preferred_el...]
    pallas_call x0 -> x1, Pallas kernels: none -> 59 us  [solve(): pl.pallas_call(functools.partial(solve_kernel, devices), out_shape=(jax.S...]
    unnamed x1 -> x0, blocking collectives: 57.6 us -> none
    all_gather x1 -> x0, blocking collectives: 24.6 us -> none  [body(): every = lax.all_gather(own_rows, 'dp', axis=0, tiled=True)]
    reduce_sum x7 -> x0, other arithmetic: 7.26 us -> none  [pieces_inner(): return lax.psum(jnp.sum(first_vec * second_vec, axis=0), 'dp')]
  transfers between devices with their start and end apart: 4 -> 0, of which waited for: 4 -> 0; matrix products, arithmetic and copies ran while one was open for 0% -> 0% of each run, Pallas kernels for 0% -> 0%
where the time goes in v1:
time: 74.6 us; the launch traced here: 74.4 us
  Pallas kernels  59 us (79%)
  other arithmetic  7.2 us (10%)
  matrix products  6.02 us (8%)
  local copies, waits for them, and re-layouts  1.42 us (2%)
  between operations  0.78 us (1%)
    pallas_call x1, Pallas kernels, solve(): pl.pallas_call(functools.partial(solve_kernel, devices), out_shape=(jax.S...  59 us
    dot_general x1, matrix products, project_rows(): jnp.dot(grad_low.reshape(ex_count * tok_count, D), proj_out, preferred_el...  4.33 us
    reduce_sum x1, other arithmetic, project_rows(): pooled = jnp.sum(live_mask * normed, axis=1) / length_float[:, 0]  2.51 us
    reduce_sum x1, other arithmetic, project_rows(): jnp.mean(hidden * hidden, axis=-1, keepdims=True) + norm_eps  2.43 us

profile of v1, /device:TPU:0, one launch (start us, length us, event | category | flops | bytes accessed | tf_op | source)
XLA Modules:
  0.0 74.4 jit_solution(15767745648395564165)
XLA Ops:
  0.6 0.0 copy-start
  0.6 0.0 copy-start.5
  0.7 0.0 copy-start.2
  0.7 0.0 copy-start.3
  0.7 0.0 copy-start.4
  0.7 0.0 copy-start.1
  0.7 0.0 copy-start.6
  0.7 0.8 %convert_element_type.27 = f32[2]{0:T(128)S(1)} convert(s32[2]{0:T(128)} %param.12) | non-fusion elementwise | flops 2 | bytes 16 | tf_op jit(solution)/shard_map/convert_element_type | solution.py:27
  1.5 2.4 %fusion.6 = f32[2,128]{1,0:T(2,128)S(1)} fusion(bf16[2,128,4096]{2,1,0:T(8,128)(2,1)} %param.11), kind=kLoop, calls=%fused_computation.10 | loop fusion | flops 3145472 | bytes 2098176 | tf_op jit(solution)/shard_map/reduce_sum | solution.py:24
  3.9 0.7 compare_convert_fusion.1
  4.7 0.7 add_sqrt_fusion
  5.4 2.5 %fusion.8 = f32[2,4096]{1,0:T(2,128)S(1)} fusion(bf16[2,128,4096]{2,1,0:T(8,128)(2,1)} %param.11, f32[2,128]{1,0:T(2,128)S(1)} %get-tuple-element.2, f32[2,128]{1,0:T(2,128)S(1)} %compare_convert_fusion.1, f32[4096]{0:T(1024)} %param.14), kind=kLoop, calls=%fused_computation.13 | loop fusion | flops 5234688 | bytes 2148352 | tf_op jit(solution)/shard_map/reduce_sum | solution.py:29
  7.9 0.0 copy-done.5
  7.9 0.4 fusion.29
  8.4 0.0 copy-done.6
  8.4 0.3 fusion.23
  8.6 0.0 copy-done
  8.7 0.0 copy-done.1
  8.7 0.8 %fusion.19 = f32[2,128,64]{1,2,0:T(8,128)S(1)} fusion(bf16[2,128,4096]{2,1,0:T(8,128)(2,1)S(1)} %copy-done, bf16[4096,64]{0,1:T(8,128)(2,1)S(1)} %copy-done.1), kind=kOutput, calls=%fused_computation.23 | convolution fusion | flops 134217728 | bytes 2686976 | tf_op jit(solution)/shard_map/dot_general | solution.py:43
  9.4 0.0 copy-done.3
  9.4 0.1 copy.12.query_ref
  9.6 0.0 copy-done.2
  9.6 0.0 copy-done.4
  9.6 4.3 %fusion.9 = f32[2,128,128]{2,1,0:T(8,128)S(1)} fusion(bf16[2,128,4096]{2,1,0:T(8,128)(2,1)} %param.11, f32[2,128]{1,0:T(2,128)S(1)} %get-tuple-element.3, f32[2,4096]{1,0:T(2,128)S(1)} %fusion.23, f32[2,128]{1,0:T(2,128)S(1)} %get-tuple-element.2, f32[2,128]{1,0:T(2,128)S(1)} %get-tuple-element.6, f32[4096]{0:T(1024)S(1)} %copy-done.2, ...), kind=kOutput, calls=%fused_computation.14 | convolution fusion | flops 281022720 | bytes 3329024 | tf_op jit(solution)/shard_map/dot_general | solution.py:48
  13.9 0.2 convolution_convert_fusion.rows_ref
  14.1 59.0 %solve.1 = (f32[512,128]{1,0:T(8,128)S(1)}, f32[2,128]{1,0:T(2,128)S(1)}) custom-call(bf16[2,64,128]{2,1,0:T(8,128)(2,1)S(1)} %convolution_convert_fusion.rows_ref, s32[128,1]{1,0:T(8,128)S(1)} %copy.12.query_ref, f32[8192,512]{1,0:T(8,128)} %prior_ref.1), custom_call_target="tpu_custom_call" | custom-call | tf_op jit(solution)/shard_map/solve/pallas_call | solution.py:405
  73.2 0.7 copy.15
  73.9 0.6 copy.16
Async XLA Ops:
  0.6 8.0 %copy-start = (bf16[2,128,4096]{2,1,0:T(8,128)(2,1)S(1)}, bf16[2,128,4096]{2,1,0:T(8,128)(2,1)}, u32[]{:S(2)}) copy-start(bf16[2,128,4096]{2,1,0:T(8,128)(2,1)} %param.10) | copy-start | bytes 6291460
  0.6 7.3 %copy-start.5 = (bf16[4096,14]{0,1:T(8,128)(2,1)S(1)}, bf16[4096,14]{0,1:T(8,128)(2,1)}, u32[]{:S(2)}) copy-start(bf16[4096,14]{0,1:T(8,128)(2,1)} %param.15) | copy-start | bytes 344068
  0.7 8.9 %copy-start.2 = (f32[4096]{0:T(1024)S(1)}, f32[4096]{0:T(1024)}, u32[]{:S(2)}) copy-start(f32[4096]{0:T(1024)} %param.14) | copy-start | bytes 49156
  0.7 8.8 %copy-start.3 = (s32[128]{0:T(128)S(1)}, s32[128]{0:T(128)}, u32[]{:S(2)}) copy-start(s32[128]{0:T(128)} %param.18) | copy-start | bytes 1540
  0.7 8.9 %copy-start.4 = (bf16[4096,128]{1,0:T(8,128)(2,1)S(1)}, bf16[4096,128]{1,0:T(8,128)(2,1)}, u32[]{:S(2)}) copy-start(bf16[4096,128]{1,0:T(8,128)(2,1)} %param.17) | copy-start | bytes 3145732
  0.7 8.0 %copy-start.1 = (bf16[4096,64]{0,1:T(8,128)(2,1)S(1)}, bf16[4096,64]{0,1:T(8,128)(2,1)}, u32[]{:S(2)}) copy-start(bf16[4096,64]{0,1:T(8,128)(2,1)} %param.16) | copy-start | bytes 1572868
  0.7 7.7 %copy-start.6 = (s32[2]{0:T(128)S(1)}, s32[2]{0:T(128)}, u32[]{:S(2)}) copy-start(s32[2]{0:T(128)} %param.13) | copy-start | bytes 28

commit v2 on v1

v2 whole, which is shorter than its diff:
```python
import functools

import jax
import jax.numpy as jnp
from jax import lax
from jax.experimental import pallas as pl
from jax.experimental.pallas import tpu as pltpu
from jax.sharding import PartitionSpec as P

ITERS = 4


norm_eps = 1e-05
damp_share = 0.5
highest = lax.Precision.HIGHEST


BASIS_SCALE = 0.125
STAGES = 4
TOKENS = 16


def split_rows(value):
    high = value.astype(jnp.bfloat16)
    rest = value - high.astype(jnp.float32)
    middle = rest.astype(jnp.bfloat16)
    low = (rest - middle.astype(jnp.float32)).astype(jnp.bfloat16)
    return jnp.concatenate([high, middle, low], axis=0)


def join_rows(value):
    part = value.shape[0] // 3
    return value[0:part] + value[part : 2 * part] + value[2 * part :]


def dot32(left, right):
    return jnp.dot(left, right, precision=highest, preferred_element_type=jnp.float32)


def solve_kernel(
    devices,
    length_ref,
    label_ref,
    gain_ref,
    query_ref,
    inputs_ref,
    outputs_ref,
    classifier_ref,
    proj_in_ref,
    proj_out_ref,
    prior_ref,
    influence_ref,
    scores_ref,
    inputs_in,
    outputs_in,
    classifier_in,
    proj_in,
    proj_out,
    root_means,
    pooled_sums,
    scaled_rows,
    grads,
    rows_all,
    rows_wide,
    vectors,
    own_vectors,
    prior_low,
    staging,
    small,
    row_out,
    row_side,
    row_pass,
    row_recv,
    vec_out,
    vec_side,
    vec_pass,
    vec_recv,
    small_send,
    small_recv,
    stage_sem,
    input_sem,
):
    me = lax.axis_index("dp")
    columns = devices // 4
    column = me // 4
    row = lax.rem(me // 2, 2)
    core = lax.rem(me, 2)
    own_count, tokens, depth = inputs_ref.shape
    feat_in = proj_in_ref.shape[1]
    feat_out = proj_out_ref.shape[1]
    total = own_count * devices
    width, piece = prior_ref.shape
    span = 4 * total
    groups_in = feat_in // devices

    fetch = [
        pltpu.make_async_copy(source, target, input_sem.at[index])
        for index, (source, target) in enumerate(
            (
                (outputs_ref, outputs_in),
                (classifier_ref, classifier_in),
                (proj_out_ref, proj_out),
                (inputs_ref, inputs_in),
                (proj_in_ref, proj_in),
            )
        )
    ]
    for copy in fetch:
        copy.start()

    def load(step):
        block = lax.rem(me + step, devices)
        return pltpu.make_async_copy(
            prior_ref.at[pl.ds(pl.multiple_of(block * piece, piece), piece)],
            staging.at[step],
            stage_sem.at[step],
        )

    def load_start(step, carry):
        load(step).start()
        return carry

    lax.fori_loop(0, devices, load_start, 0)

    barrier = pltpu.get_barrier_semaphore()

    def greet(step, carry):
        pl.semaphore_signal(
            barrier, inc=1, device_id={"dp": lax.rem(me + step, devices)}
        )
        return carry

    lax.fori_loop(1, devices, greet, 0)

    blocks = tokens // TOKENS

    def live_of(example, start):
        positions = lax.broadcasted_iota(jnp.int32, (TOKENS, 1), 0) + start
        return (positions < length_ref[example]).astype(jnp.float32)

    scaled_rows[...] = jnp.zeros_like(scaled_rows)
    fetch[0].wait()
    for example in range(own_count):

        def pool(block, carry, example=example):
            start = pl.multiple_of(block * TOKENS, TOKENS)
            hidden = outputs_in[example, pl.ds(start, TOKENS), :].astype(jnp.float32)
            root_mean = jnp.sqrt(
                jnp.sum(hidden * hidden, axis=1, keepdims=True) / depth + norm_eps
            )
            root_means[example, pl.ds(start, TOKENS), :] = root_mean
            term = hidden * (live_of(example, start) / root_mean)
            pooled_sums[...] += jnp.sum(term.reshape(TOKENS // 8, 8, depth), axis=0)
            return carry

        pooled_sums[...] = jnp.zeros_like(pooled_sums)
        lax.fori_loop(0, blocks, pool, 0)
        scaled_rows[example : example + 1, :] = (
            gain_ref[...]
            * jnp.sum(pooled_sums[...], axis=0, keepdims=True)
            / length_ref[example].astype(jnp.float32)
        )

    fetch[1].wait()
    logits = join_rows(
        jnp.dot(
            split_rows(scaled_rows[...]), classifier_in[...], preferred_element_type=jnp.float32
        )
    )
    exponent = jnp.exp(logits)
    probs = exponent / jnp.sum(exponent, axis=1, keepdims=True)
    row_ids = lax.broadcasted_iota(jnp.int32, probs.shape, 0)
    class_ids = lax.broadcasted_iota(jnp.int32, probs.shape, 1)
    difference = probs
    for example in range(own_count):
        difference = difference - (
            (row_ids == example) & (class_ids == label_ref[example])
        ).astype(jnp.float32)
    pooled_grad = join_rows(
        lax.dot_general(
            split_rows(difference),
            classifier_in[...],
            (((1,), (1,)), ((), ())),
            preferred_element_type=jnp.float32,
        )
    )
    for example in range(own_count):
        scaled_rows[example : example + 1, :] = (
            gain_ref[...]
            * (1.0 / length_ref[example].astype(jnp.float32))
            * pooled_grad[example : example + 1, :]
        )

    for index in (2, 3, 4):
        fetch[index].wait()
    for example in range(own_count):

        def differentiate(block, carry, example=example):
            start = pl.multiple_of(block * TOKENS, TOKENS)
            hidden = outputs_in[example, pl.ds(start, TOKENS), :].astype(jnp.float32)
            root_mean = root_means[example, pl.ds(start, TOKENS), :]
            live = live_of(example, start)
            scaled = scaled_rows[example : example + 1, :]
            along = live * jnp.sum(hidden * scaled, axis=1, keepdims=True)
            along = along / (depth * root_mean * root_mean * root_mean)
            grads[pl.ds(start, TOKENS), :] = (
                scaled * (live / root_mean) - hidden * along
            ).astype(jnp.bfloat16)
            return carry

        lax.fori_loop(0, blocks, differentiate, 0)
        grad_proj = jnp.dot(grads[...], proj_out[...], preferred_element_type=jnp.float32)
        input_proj = jnp.dot(
            inputs_in[example], proj_in[...], preferred_element_type=jnp.float32
        )
        rows_all[me * own_count + example] = lax.dot_general(
            input_proj,
            grad_proj,
            (((0,), (0,)), ((), ())),
            precision=highest,
            preferred_element_type=jnp.float32,
        ).astype(jnp.bfloat16)

    pl.semaphore_wait(barrier, devices - 1)

    def send(view, sem_out, sem_in, target):
        return pltpu.make_async_remote_copy(
            src_ref=view,
            dst_ref=view,
            send_sem=sem_out,
            recv_sem=sem_in,
            device_id={"dp": target},
        )

    def row_view(source):
        return rows_all.at[pl.ds(source * own_count, own_count)]

    def row_copy(source, sem_out, target):
        return send(row_view(source), sem_out, row_recv.at[source], target)

    def vec_copy(stage, source, sem_out, target):
        view = vectors.at[source, pl.ds(stage * total, total)]
        return send(view, sem_out, vec_recv.at[stage, source], target)

    def device_at(step, other_row, other_core):
        at = lax.rem(column + columns + step, columns)
        return at * 4 + (1 - row if other_row else row) * 2 + (1 - core if other_core else core)

    side = device_at(0, True, False)
    sibling = device_at(0, False, True)

    def gather_start(copy, out, over, on):
        copy(me, over(0), side).start()

        def push(step, carry):
            copy(me, out(step), device_at(step, False, False)).start()
            return carry

        lax.fori_loop(1, columns, push, 0)
        copy(me, on(0), sibling).start()

    def gather(copy, out, over, on, use, state):
        state = use(me, state)

        def take_column(step, carry):
            source = device_at(-step, False, False)
            copy(source, on(step), sibling).wait_recv()
            copy(source, over(step), side).start()
            copy(source, on(step), sibling).start()
            return use(source, carry)

        state = lax.fori_loop(1, columns, take_column, state)

        def take_side(step, carry):
            source = device_at(-step, True, False)
            copy(source, on(columns + step), sibling).wait_recv()
            copy(source, on(columns + step), sibling).start()
            return use(source, carry)

        state = lax.fori_loop(0, columns, take_side, state)

        def take_core(step, carry):
            for other_row in (False, True):
                source = device_at(-step, other_row, True)
                copy(source, on(step), sibling).wait_recv()
                carry = use(source, carry)
            return carry

        return lax.fori_loop(0, columns, take_core, state)

    def drain(copy, out, over, on):
        def finish(step, carry):
            copy(device_at(-step, False, False), over(step), side).wait_send()
            copy(device_at(-step, False, False), on(step), sibling).wait_send()
            copy(device_at(-step, True, False), on(columns + step), sibling).wait_send()
            return carry

        lax.fori_loop(0, columns, finish, 0)

        def finish_column(step, carry):
            copy(me, out(step), device_at(step, False, False)).wait_send()
            return carry

        lax.fori_loop(1, columns, finish_column, 0)

    def small_copy(turn, step, source, target):
        return send(
            small.at[turn, source], small_send.at[turn, step], small_recv.at[turn, source], target
        )

    def small_push(turn):
        def push(step, carry):
            small_copy(turn, step, me, lax.rem(me + step, devices)).start()
            return carry

        lax.fori_loop(1, devices, push, 0)

    def small_sum(turn):
        def finish(step, carry):
            source = lax.rem(me + devices - step, devices)
            small_copy(turn, step, source, source).wait_recv()
            small_copy(turn, step, me, source).wait_send()
            return carry

        lax.fori_loop(1, devices, finish, 0)
        return jnp.sum(small[turn], axis=0)

    def sems(array, *at):
        return lambda step: array.at[(*at, step)]

    row_sems = (row_copy, sems(row_out), sems(row_side), sems(row_pass))
    gather_start(*row_sems)

    load(0).wait()
    block = staging[0]
    on_diag = lax.broadcasted_iota(jnp.int32, (piece, piece), 0) == lax.broadcasted_iota(
        jnp.int32, (piece, piece), 1
    )
    diag = jnp.sum(jnp.where(on_diag, block, 0.0), axis=0, keepdims=True)
    prior_low[me] = jnp.where(on_diag, 0.0, block).astype(jnp.bfloat16)
    small[0, me] = jnp.full(small.shape[2:], jnp.sum(diag) / width, jnp.float32)
    small_push(0)

    def cast(step, carry):
        load(step).wait()
        prior_low[lax.rem(me + step, devices)] = staging[step].astype(jnp.bfloat16)
        return carry

    def use_rows(source, step):
        @pl.when(step > 0)
        def _():
            cast(step, 0)

        return step + 1

    gather(*row_sems, use_rows, 0)

    def widen(step, carry):
        rows_wide[pl.ds(pl.multiple_of(step * feat_in, feat_in), feat_in)] = rows_all[
            step
        ].astype(jnp.float32)
        return carry

    lax.fori_loop(0, total, widen, 0)
    for index in range(feat_in):
        vectors[
            index // groups_in,
            0:total,
            (index % groups_in) * feat_out : (index % groups_in + 1) * feat_out,
        ] = rows_wide[pl.ds(index, total, stride=feat_in), :].astype(jnp.bfloat16)

    shift = small_sum(0)[0:1, 0:1]
    diag = diag - shift

    def partial(stage):
        def use(source, acc):
            return acc + jnp.dot(
                vectors[source, stage * total : (stage + 1) * total, :],
                prior_low[source],
                preferred_element_type=jnp.float32,
            )

        return use

    def next_vector(stage, acc):
        return BASIS_SCALE * (acc + diag * own_vectors[stage * total : (stage + 1) * total, :])

    def vec_sems(stage):
        return (
            functools.partial(vec_copy, stage),
            sems(vec_out, stage),
            sems(vec_side, stage),
            sems(vec_pass, stage),
        )

    zero = jnp.zeros((total, piece), jnp.float32)
    own_vectors[0:total, :] = vectors[me, 0:total, :].astype(jnp.float32)
    acc = lax.fori_loop(0, devices, partial(0), zero)
    for stage in range(1, STAGES):
        fresh = next_vector(stage - 1, acc)
        own_vectors[stage * total : (stage + 1) * total, :] = fresh
        vectors[me, stage * total : (stage + 1) * total, :] = fresh.astype(jnp.bfloat16)
        gather_start(*vec_sems(stage))
        acc = gather(*vec_sems(stage), partial(stage), zero)
    last = next_vector(STAGES - 1, acc)
    product = last * own_vectors[3 * total :, :]
    small[1, me] = lax.dot_general(
        jnp.ones((8, piece), jnp.float32),
        product,
        (((1,), (1,)), ((), ())),
        precision=highest,
        preferred_element_type=jnp.float32,
    )
    small_push(1)

    def add_gram(source, acc):
        block = vectors[source]
        return acc + lax.dot_general(
            block, block, (((1,), (1,)), ((), ())), preferred_element_type=jnp.float32
        )

    gram = lax.fori_loop(0, devices, add_gram, jnp.zeros((span, span), jnp.float32))

    row_ids = lax.broadcasted_iota(jnp.int32, (span, span), 0)
    col_ids = lax.broadcasted_iota(jnp.int32, (span, span), 1)
    trace = jnp.sum(
        jnp.sum(
            jnp.where((row_ids == col_ids) & (row_ids < total), gram, 0.0), axis=0, keepdims=True
        ),
        axis=1,
        keepdims=True,
    )
    damping = damp_share * trace / (total * total)
    lower = damping * shift
    raise_ = damping / BASIS_SCALE
    lanes = lax.broadcasted_iota(jnp.int32, (total, span), 1)
    start = (lanes == lax.broadcasted_iota(jnp.int32, (total, span), 0)).astype(jnp.float32)
    final_lanes = lanes >= 3 * total

    def shift_up(coeffs):
        return jnp.where(lanes >= total, pltpu.roll(coeffs, total, 1), 0.0)

    def inner(left, right):
        return jnp.sum(left * right, axis=1, keepdims=True)

    solved = jnp.zeros((total, span), jnp.float32)
    residual = start
    direction = start
    projected = dot32(start, gram)
    norm_now = inner(projected, residual)
    for step in range(ITERS):
        moved = shift_up(direction)
        image = (
            jnp.where(lanes < total, projected / total, 0.0) + lower * direction + raise_ * moved
        )
        energy = inner(projected, image)
        if step == ITERS - 1:
            tail = jnp.where(final_lanes, direction, 0.0)
            energy = energy + raise_ * inner(dot32(moved, gram), tail)
            sevenths = small_sum(1)[0:1, :]
            pick = (
                lax.broadcasted_iota(jnp.int32, (total, total), 0)
                == lax.broadcasted_iota(jnp.int32, (total, total), 1)
            )
            seventh = jnp.sum(jnp.where(pick, sevenths, 0.0), axis=1, keepdims=True)
            energy = energy + raise_ * seventh * inner(tail, tail)
        alpha = norm_now / energy
        solved = solved + alpha * direction
        if step < ITERS - 1:
            residual = residual - alpha * image
            pulled = dot32(residual, gram)
            norm_next = inner(pulled, residual)
            ratio = norm_next / norm_now
            direction = residual + ratio * direction
            projected = pulled + ratio * projected
            norm_now = norm_next

    queries = query_ref.shape[0]
    chosen = (
        query_ref[...] == lax.broadcasted_iota(jnp.int32, (queries, total), 1)
    ).astype(jnp.float32)
    picked = dot32(chosen, solved)
    influence_ref[...] = dot32(picked, own_vectors[...]).T
    own_ids = lax.broadcasted_iota(jnp.int32, (8, span), 0) + me * own_count
    own_rows = (
        (own_ids == lax.broadcasted_iota(jnp.int32, (8, span), 1))
        & (lax.broadcasted_iota(jnp.int32, (8, span), 0) < own_count)
    ).astype(jnp.float32)
    shares = dot32(own_rows, gram)
    scored = lax.dot_general(
        shares,
        picked,
        (((1,), (1,)), ((), ())),
        precision=highest,
        preferred_element_type=jnp.float32,
    )
    scores_ref[...] = scored[0:own_count, :] / total

    drain(*row_sems)
    for stage in range(1, STAGES):
        drain(*vec_sems(stage))


def body(
    inputs,
    outputs,
    lengths,
    labels,
    norm_gain,
    classifier,
    proj_in,
    proj_out,
    query_index,
    prior_fisher,
):
    devices = lax.axis_size("dp")
    own_count, tokens, depth = inputs.shape
    feat_in, feat_out = proj_in.shape[1], proj_out.shape[1]
    width, piece = prior_fisher.shape
    total = own_count * devices
    queries = query_index.shape[0]
    columns = devices // 4
    vmem = pl.BlockSpec(memory_space=pltpu.VMEM)
    smem = pl.BlockSpec(memory_space=pltpu.SMEM)
    hbm = pl.BlockSpec(memory_space=pl.ANY)
    dma = pltpu.SemaphoreType.DMA
    return pl.pallas_call(
        functools.partial(solve_kernel, devices),
        out_shape=(
            jax.ShapeDtypeStruct((piece, queries), jnp.float32),
            jax.ShapeDtypeStruct((own_count, queries), jnp.float32),
        ),
        in_specs=[smem, smem, vmem, vmem, hbm, hbm, hbm, hbm, hbm, hbm],
        out_specs=(vmem, vmem),
        scratch_shapes=[
            pltpu.VMEM(inputs.shape, jnp.bfloat16),
            pltpu.VMEM(outputs.shape, jnp.bfloat16),
            pltpu.VMEM(classifier.shape, jnp.bfloat16),
            pltpu.VMEM(proj_in.shape, jnp.bfloat16),
            pltpu.VMEM(proj_out.shape, jnp.bfloat16),
            pltpu.VMEM((own_count, tokens, 1), jnp.float32),
            pltpu.VMEM((8, depth), jnp.float32),
            pltpu.VMEM((8, depth), jnp.float32),
            pltpu.VMEM((tokens, depth), jnp.bfloat16),
            pltpu.VMEM((total, feat_in, feat_out), jnp.bfloat16),
            pltpu.VMEM((total * feat_in, feat_out), jnp.float32),
            pltpu.VMEM((devices, 4 * total, piece), jnp.bfloat16),
            pltpu.VMEM((4 * total, piece), jnp.float32),
            pltpu.VMEM((devices, piece, piece), jnp.bfloat16),
            pltpu.VMEM((devices, piece, piece), jnp.float32),
            pltpu.VMEM((2, devices, 8, total), jnp.float32),
            dma((columns,)),
            dma((columns,)),
            dma((2 * columns,)),
            dma((devices,)),
            dma((STAGES, columns)),
            dma((STAGES, columns)),
            dma((STAGES, 2 * columns)),
            dma((STAGES, devices)),
            dma((2, devices)),
            dma((2, devices)),
            dma((devices,)),
            dma((5,)),
        ],
        compiler_params=pltpu.CompilerParams(
            collective_id=0, has_side_effects=True, vmem_limit_bytes=56 * 1024 * 1024
        ),
        name="solve",
    )(
        lengths,
        labels,
        norm_gain[None],
        query_index[:, None],
        inputs,
        outputs,
        classifier,
        proj_in,
        proj_out,
        prior_fisher,
    )


def solution(mesh):
    return jax.shard_map(
        body,
        mesh=mesh,
        in_specs=(
            P(("groups", "dp"), None, None),
            P(("groups", "dp"), None, None),
            P(("groups", "dp")),
            P(("groups", "dp")),
            P(),
            P(),
            P(),
            P(),
            P("groups"),
            P("groups", "dp"),
        ),
        out_specs=(P("dp", "groups"), P(("groups", "dp"), None)),
        check_vma=False,
    )
```

time: 74.6 us -> 74.6 us (level)
  local copies, waits for them, and re-layouts: 1.42 us -> 9.01 us
  other arithmetic: 7.2 us -> 0 us
  matrix products: 6.02 us -> 0 us
  Pallas kernels: 59 us -> 64.7 us
    unnamed x16 -> x4, local copies, waits for them, and re-layouts: 1.3 us -> 7.62 us
    dot_general x5 -> x0, matrix products: 6.02 us -> none  [the longest x1 4.33 us: project_rows(): jnp.dot(grad_low.reshape(ex_count * tok_count, D), proj_out, preferred_el...]
    pallas_call x1, Pallas kernels: 59 us -> 64.7 us  [body(): pl.pallas_call(functools.partial(solve_kernel, devices), out_shape=(jax.S...]
    reduce_sum x2 -> x0, other arithmetic: 4.94 us -> none  [the longest x1 2.51 us: project_rows(): pooled = jnp.sum(live_mask * normed, axis=1) / length_float[:, 0]]
    convert_element_type x2 -> x0, other arithmetic: 1.54 us -> none  [the longest x1 0.81 us: project_rows(): length_float = lengths.astype(jnp.float32)[:, None, None]]
    broadcast_in_dim x1, local copies, waits for them, and re-layouts: 0.11 us -> 1.39 us  [body(): query_index[:, None]]
where the time goes in v2:
time: 74.6 us; the launch traced here: 74.3 us
  Pallas kernels  64.7 us (87%)
  local copies, waits for them, and re-layouts  9.01 us (12%)
    pallas_call x1, Pallas kernels, body(): pl.pallas_call(functools.partial(solve_kernel, devices), out_shape=(jax.S...  64.7 us
    unnamed x4, local copies, waits for them, and re-layouts  7.62 us

profile of v2, /device:TPU:0, one launch (start us, length us, event | category | flops | bytes accessed | tf_op | source)
XLA Modules:
  0.0 74.3 jit_solution(385987044539251417)
XLA Ops:
  0.6 1.4 %copy.12.query_ref = s32[128,1]{1,0:T(8,128)} copy(s32[128,1]{0,1:T(1,128)} %bitcast.3) | data formatting | bytes 1024 | tf_op jit(solution)/shard_map/broadcast_in_dim | solution.py:573
  2.0 2.3 %copy.13.classifier_ref = bf16[4096,14]{1,0:T(8,128)(2,1)} copy(bf16[4096,14]{0,1:T(8,128)(2,1)} %param.15) | data formatting | bytes 229376 | tf_op args[5]
  4.3 2.4 %copy.14.proj_in_ref = bf16[4096,64]{1,0:T(8,128)(2,1)} copy(bf16[4096,64]{0,1:T(8,128)(2,1)} %param.16) | data formatting | bytes 1048576 | tf_op args[6]
  6.7 64.7 %solve.1 = (f32[512,128]{1,0:T(8,128)}, f32[2,128]{1,0:T(2,128)}) custom-call(s32[2]{0:T(128)} %length_ref.1, s32[2]{0:T(128)} %label_ref.1, f32[1,4096]{1,0:T(1,128)} %bitcast.2, s32[128,1]{1,0:T(8,128)} %copy.12.query_ref, bf16[2,128,4096]{2,1,0:T(8,128)(2,1)} %inputs_ref.1, bf16[2,128,4096]{2,1,0:T(8,128)(2,1)} %outputs_ref.1, ...), custom_call_target="tpu_custom_call" | custom-call | tf_op jit(solution)/shard_map/solve/pallas_call | solution.py:527
  71.4 1.7 %copy.17 = f32[512,128]{1,0:T(8,128)} copy(f32[512,128]{1,0:T(8,128)} %get-tuple-element.4) | data formatting | bytes 524288
  73.1 1.2 %copy.18 = f32[2,128]{1,0:T(2,128)} copy(f32[2,128]{1,0:T(2,128)} %get-tuple-element.5) | data formatting | bytes 2048

commit v3 on v2

--- a/solution.py
+++ b/solution.py
@@ -42,15 +42,15 @@
     length_ref,
     label_ref,
     gain_ref,
-    query_ref,
     inputs_ref,
     outputs_ref,
     classifier_ref,
     proj_in_ref,
     proj_out_ref,
     prior_ref,
-    influence_ref,
-    scores_ref,
+    solved_ref,
+    own_vectors,
+    shares_ref,
     inputs_in,
     outputs_in,
     classifier_in,
@@ -63,7 +63,6 @@
     rows_all,
     rows_wide,
     vectors,
-    own_vectors,
     prior_low,
     staging,
     small,
@@ -86,7 +85,7 @@
     row = lax.rem(me // 2, 2)
     core = lax.rem(me, 2)
     own_count, tokens, depth = inputs_ref.shape
-    feat_in = proj_in_ref.shape[1]
+    feat_in = proj_in_ref.shape[0]
     feat_out = proj_out_ref.shape[1]
     total = own_count * devices
     width, piece = prior_ref.shape
@@ -163,8 +162,11 @@
 
     fetch[1].wait()
     logits = join_rows(
-        jnp.dot(
-            split_rows(scaled_rows[...]), classifier_in[...], preferred_element_type=jnp.float32
+        lax.dot_general(
+            split_rows(scaled_rows[...]),
+            classifier_in[...],
+            (((1,), (1,)), ((), ())),
+            preferred_element_type=jnp.float32,
         )
     )
     exponent = jnp.exp(logits)
@@ -177,12 +179,7 @@
             (row_ids == example) & (class_ids == label_ref[example])
         ).astype(jnp.float32)
     pooled_grad = join_rows(
-        lax.dot_general(
-            split_rows(difference),
-            classifier_in[...],
-            (((1,), (1,)), ((), ())),
-            preferred_element_type=jnp.float32,
-        )
+        jnp.dot(split_rows(difference), classifier_in[...], preferred_element_type=jnp.float32)
     )
     for example in range(own_count):
         scaled_rows[example : example + 1, :] = (
@@ -210,16 +207,13 @@
 
         lax.fori_loop(0, blocks, differentiate, 0)
         grad_proj = jnp.dot(grads[...], proj_out[...], preferred_element_type=jnp.float32)
-        input_proj = jnp.dot(
-            inputs_in[example], proj_in[...], preferred_element_type=jnp.float32
-        )
-        rows_all[me * own_count + example] = lax.dot_general(
-            input_proj,
-            grad_proj,
-            (((0,), (0,)), ((), ())),
-            precision=highest,
+        input_proj = lax.dot_general(
+            proj_in[...],
+            inputs_in[example],
+            (((1,), (1,)), ((), ())),
             preferred_element_type=jnp.float32,
-        ).astype(jnp.bfloat16)
+        )
+        rows_all[me * own_count + example] = dot32(input_proj, grad_proj).astype(jnp.bfloat16)
 
     pl.semaphore_wait(barrier, devices - 1)
 
@@ -475,30 +469,28 @@
             projected = pulled + ratio * projected
             norm_now = norm_next
 
-    queries = query_ref.shape[0]
-    chosen = (
-        query_ref[...] == lax.broadcasted_iota(jnp.int32, (queries, total), 1)
-    ).astype(jnp.float32)
-    picked = dot32(chosen, solved)
-    influence_ref[...] = dot32(picked, own_vectors[...]).T
+    solved_ref[...] = solved
     own_ids = lax.broadcasted_iota(jnp.int32, (8, span), 0) + me * own_count
     own_rows = (
         (own_ids == lax.broadcasted_iota(jnp.int32, (8, span), 1))
         & (lax.broadcasted_iota(jnp.int32, (8, span), 0) < own_count)
     ).astype(jnp.float32)
-    shares = dot32(own_rows, gram)
-    scored = lax.dot_general(
-        shares,
-        picked,
-        (((1,), (1,)), ((), ())),
-        precision=highest,
-        preferred_element_type=jnp.float32,
-    )
-    scores_ref[...] = scored[0:own_count, :] / total
+    shares_ref[...] = dot32(own_rows, gram) / total
 
     drain(*row_sems)
     for stage in range(1, STAGES):
         drain(*vec_sems(stage))
+
+
+def finish_kernel(query_ref, solved_ref, own_vectors_ref, shares_ref, influence_ref, scores_ref):
+    total = solved_ref.shape[0]
+    queries = query_ref.shape[1]
+    chosen = (
+        lax.broadcasted_iota(jnp.int32, (total, queries), 0) == query_ref[...]
+    ).astype(jnp.float32)
+    picked = dot32(solved_ref[...].T, chosen)
+    influence_ref[...] = dot32(own_vectors_ref[...].T, picked)
+    scores_ref[...] = dot32(shares_ref[...], picked)[0 : scores_ref.shape[0], :]
 
 
 def body(
@@ -524,19 +516,20 @@
     smem = pl.BlockSpec(memory_space=pltpu.SMEM)
     hbm = pl.BlockSpec(memory_space=pl.ANY)
     dma = pltpu.SemaphoreType.DMA
-    return pl.pallas_call(
+    parts = pl.pallas_call(
         functools.partial(solve_kernel, devices),
         out_shape=(
-            jax.ShapeDtypeStruct((piece, queries), jnp.float32),
-            jax.ShapeDtypeStruct((own_count, queries), jnp.float32),
+            jax.ShapeDtypeStruct((total, 4 * total), jnp.float32),
+            jax.ShapeDtypeStruct((4 * total, piece), jnp.float32),
+            jax.ShapeDtypeStruct((8, 4 * total), jnp.float32),
         ),
-        in_specs=[smem, smem, vmem, vmem, hbm, hbm, hbm, hbm, hbm, hbm],
-        out_specs=(vmem, vmem),
+        in_specs=[smem, smem, vmem, hbm, hbm, hbm, hbm, hbm, hbm],
+        out_specs=(vmem, vmem, vmem),
         scratch_shapes=[
             pltpu.VMEM(inputs.shape, jnp.bfloat16),
             pltpu.VMEM(outputs.shape, jnp.bfloat16),
-            pltpu.VMEM(classifier.shape, jnp.bfloat16),
-            pltpu.VMEM(proj_in.shape, jnp.bfloat16),
+            pltpu.VMEM(classifier.shape[::-1], jnp.bfloat16),
+            pltpu.VMEM(proj_in.shape[::-1], jnp.bfloat16),
             pltpu.VMEM(proj_out.shape, jnp.bfloat16),
             pltpu.VMEM((own_count, tokens, 1), jnp.float32),
             pltpu.VMEM((8, depth), jnp.float32),
@@ -545,7 +538,6 @@
             pltpu.VMEM((total, feat_in, feat_out), jnp.bfloat16),
             pltpu.VMEM((total * feat_in, feat_out), jnp.float32),
             pltpu.VMEM((devices, 4 * total, piece), jnp.bfloat16),
-            pltpu.VMEM((4 * total, piece), jnp.float32),
             pltpu.VMEM((devices, piece, piece), jnp.bfloat16),
             pltpu.VMEM((devices, piece, piece), jnp.float32),
             pltpu.VMEM((2, devices, 8, total), jnp.float32),
@@ -570,14 +562,23 @@
         lengths,
         labels,
         norm_gain[None],
-        query_index[:, None],
         inputs,
         outputs,
-        classifier,
-        proj_in,
+        classifier.T,
+        proj_in.T,
         proj_out,
         prior_fisher,
     )
+    return pl.pallas_call(
+        finish_kernel,
+        out_shape=(
+            jax.ShapeDtypeStruct((piece, queries), jnp.float32),
+            jax.ShapeDtypeStruct((own_count, queries), jnp.float32),
+        ),
+        in_specs=[vmem] * 4,
+        out_specs=(vmem, vmem),
+        name="finish",
+    )(query_index[None], *parts)
 
 
 def solution(mesh):

time: 74.6 us -> 67.5 us (0.905)
  local copies, waits for them, and re-layouts: 9.01 us -> 0 us
  Pallas kernels: 64.7 us -> 66.6 us
    unnamed x4 -> x0, local copies, waits for them, and re-layouts: 7.62 us -> none
    pallas_call x0 -> x1, Pallas kernels: none -> 2.44 us  [body(): pl.pallas_call(finish_kernel, out_shape=(jax.ShapeDtypeStruct((piece, que...]
    broadcast_in_dim x1 -> x0, local copies, waits for them, and re-layouts: 1.39 us -> none  [body(): query_index[:, None]]
where the time goes in v3:
time: 67.5 us; the launch traced here: 67.2 us
  Pallas kernels  66.6 us (99%)
    pallas_call x1, Pallas kernels, body(): pl.pallas_call(functools.partial(solve_kernel, devices), out_shape=(jax.S...  64.2 us
    pallas_call x1, Pallas kernels, body(): pl.pallas_call(finish_kernel, out_shape=(jax.ShapeDtypeStruct((piece, que...  2.44 us

profile of v3, /device:TPU:0, one launch (start us, length us, event | category | flops | bytes accessed | tf_op | source)
XLA Modules:
  0.0 67.2 jit_solution(12306761443389239994)
XLA Ops:
  0.6 64.2 %solve.1 = (f32[32,128]{1,0:T(8,128)}, f32[128,512]{1,0:T(8,128)}, f32[8,128]{1,0:T(8,128)}) custom-call(s32[2]{0:T(128)} %length_ref.1, s32[2]{0:T(128)} %label_ref.1, f32[1,4096]{1,0:T(1,128)} %bitcast.6, bf16[2,128,4096]{2,1,0:T(8,128)(2,1)} %inputs_ref.1, bf16[2,128,4096]{2,1,0:T(8,128)(2,1)} %outputs_ref.1, bf16[14,4096]{1,0:T(8,128)(2,1)} %bitcast.5, ...), custom_call_target="tpu_custom_call" | custom-call | tf_op jit(solution)/shard_map/solve/pallas_call | solution.py:519
  64.8 2.4 %finish.1 = (f32[512,128]{1,0:T(8,128)}, f32[2,128]{1,0:T(2,128)}) custom-call(s32[1,128]{1,0:T(1,128)} %bitcast.7, f32[32,128]{1,0:T(8,128)} %get-tuple-element.5.solved_ref, f32[128,512]{1,0:T(8,128)} %get-tuple-element.6.own_vectors_ref, f32[8,128]{1,0:T(8,128)} %get-tuple-element.7.shares_ref), custom_call_target="tpu_custom_call" | custom-call | tf_op jit(solution)/shard_map/finish/pallas_call | solution.py:572
